TPU v7x, 512 devices: a whole 4x4x16 slice. The times are simulated.
512 devices in a mesh: dp: 128 (over z_lo, x, y, core), section: 4 (over z_hi).
Axes of the slice: x: 4, y: 4, z: 16 (z_hi: 4, z_lo: 4; z = z_hi * 4 + z_lo), core: 2. Of those that a mesh axis runs over, the one named last changes fastest.
Arguments:
- saved_inputs: bfloat16 [4, 2, 768, 6144], P('section', None, 'dp'), may hold values from -6 to 6
- carried: bfloat16 [4, 768, 6144], P('section', 'dp'), may hold values from -6 to 6
- head_grad: bfloat16 [768, 6144], P('dp'), may hold values from -6 to 6
- routing: int32 [4, 2, 768, 2], P('section', None, 'dp'), may hold values from 0 to 7, as said below
- replica_counts: int32 [128], replicated, may hold values from 2 to 5
- router: float32 [4, 6144, 8], P('section'), may hold values from -0.21875 to 0.21875
- w_in: bfloat16 [4, 128, 1536, 256], P('section', 'dp'), may hold values from -0.078125 to 0.078125
- w_out: bfloat16 [4, 128, 256, 1536], P('section', 'dp'), may hold values from -0.0625 to 0.0625
Outputs:
- input_grad: bfloat16 [2, 4, 768, 6144], P(None, 'section', 'dp')
- grad_in: bfloat16 [4, 128, 1536, 256], P('section', 'dp')
- grad_out: bfloat16 [4, 128, 256, 1536], P('section', 'dp')
- grad_router: float32 [4, 6144, 8], P('section')
Inputs may be any that keep to these rules, and one draw needn't show every extreme that they name: `routing`: each row names 2 different experts; in every section and step at most 2 of one device's 6 tokens name expert 0, and exactly 2 on some device.
All inputs are finite; a program needn't handle non-finite values.
Results may differ from a plain program's by a relative error of at most 0.0057.
Values may be sent and summed in bfloat16 or wider, within the bound.
A program may use at most 64 MiB of HBM per device.

v0:
```python
import jax
import jax.numpy as jnp
from jax import lax
from jax.sharding import PartitionSpec as P

STEPS = 2
CAP = 2


def shifted(array, axis, by):
    devices = lax.axis_size(axis)
    pairs = [(i, i + by) for i in range(devices) if 0 <= i + by < devices]
    return lax.ppermute(array, axis, pairs)


def from_partner(block, axis, distance):
    count = lax.axis_size(axis)
    route = []
    for low in range(count):
        high = low | 1 << distance
        if high != low and high < count:
            route += [(low, high), (high, low)]
    return lax.ppermute(block, axis, route)


def silu_grad(value):
    sig = jax.nn.sigmoid(value)
    return sig * (1.0 + value * (1.0 - sig))


def local(saved_inputs, carried, head_grad, routing, replica_counts, router, w_in, w_out):
    hi = lax.Precision.HIGHEST
    section_count = lax.axis_size("section")
    section_index = lax.axis_index("section")
    dev_count = lax.axis_size("dp")
    dev_index = lax.axis_index("dp")
    groups = dev_count // 4
    width = head_grad.shape[1]
    part = w_in.shape[2]
    hidden = w_in.shape[3]
    experts = router.shape[2]
    rows = dev_count * CAP
    weight_in = w_in[0, 0]
    weight_out = w_out[0, 0]
    router_w = router[0]
    quarter = dev_index % 4
    my_count = replica_counts[dev_index]
    first = (jnp.arange(experts) == 0).astype(jnp.float32)
    slots = jnp.arange(CAP, dtype=jnp.int32)

    def prepare(step):
        xin = saved_inputs[0, step]
        ids = routing[0, step]
        live = step + section_index < my_count
        xf = xin.astype(jnp.float32)
        logits = jnp.dot(xf, router_w, precision=hi)
        expo = jnp.exp(logits)
        prob = expo / jnp.sum(expo, axis=1, keepdims=True)
        routed = ((ids[:, 0] == 0) | (ids[:, 1] == 0)) & live
        flags = routed.astype(jnp.int32)
        slot = jnp.cumsum(flags, dtype=jnp.int32) - 1
        table = ((slot[None, :] == slots[:, None]) & routed[None, :]).astype(jnp.float32)
        xs = jnp.dot(table.astype(jnp.bfloat16), xin, preferred_element_type=jnp.float32).astype(
            jnp.bfloat16
        )
        gate = jnp.dot(table, prob[:, 0], precision=hi).astype(jnp.bfloat16)
        xsend = jnp.broadcast_to(
            xs.reshape(CAP, 4, part).transpose(1, 0, 2)[None], (groups, 4, CAP, part)
        ).reshape(dev_count, CAP, part)
        gsend = jnp.broadcast_to(gate[None], (dev_count, CAP))
        return (xf, prob, table, live, xsend, gsend)

    prepared = [prepare(step) for step in range(STEPS)]
    acc_in = jnp.zeros((part, hidden), jnp.float32)
    acc_out = jnp.zeros((hidden, part), jnp.float32)
    acc_router = jnp.zeros((width, experts), jnp.float32)
    outputs = []
    incoming = carried[0]
    for step in range(STEPS):
        xf, prob, table, live, xsend, gsend = prepared[step]
        if step == 1:
            passed = shifted(outputs[0], "section", -1)
            incoming = jnp.where(section_index == section_count - 1, head_grad, passed)
        grad_in_tok = jnp.where(live, incoming, jnp.zeros_like(incoming))
        ys = jnp.dot(
            table.astype(jnp.bfloat16), grad_in_tok, preferred_element_type=jnp.float32
        ).astype(jnp.bfloat16)
        ysend = jnp.broadcast_to(
            ys.reshape(CAP, 4, part).transpose(1, 0, 2)[None], (groups, 4, CAP, part)
        ).reshape(dev_count, CAP, part)
        recv_x, recv_y, recv_g = (
            lax.all_to_all(xsend, "dp", split_axis=0, concat_axis=0, tiled=True),
            lax.all_to_all(ysend, "dp", split_axis=0, concat_axis=0, tiled=True),
            lax.all_to_all(gsend, "dp", split_axis=0, concat_axis=0, tiled=True),
        )
        rows_x = recv_x.reshape(rows, part)
        rows_y = recv_y.reshape(rows, part)
        gate_f = recv_g.reshape(rows).astype(jnp.float32)[:, None]
        pre = jnp.dot(rows_x, weight_in, preferred_element_type=jnp.float32)
        upper = lax.dot_general(
            rows_y, weight_out, (((1,), (1,)), ((), ())), preferred_element_type=jnp.float32
        )
        for bit in range(2):
            other_pre, other_upper = from_partner((pre, upper), "dp", bit)
            pre = pre + other_pre
            upper = upper + other_upper
        act = jax.nn.silu(pre)
        dpre = (gate_f * upper * silu_grad(pre)).astype(jnp.bfloat16)
        scaled = (gate_f * act).astype(jnp.bfloat16)
        block_sum = jnp.sum(act * upper, axis=1)
        block_sum = jnp.where(quarter == 0, block_sum, jnp.zeros_like(block_sum)).astype(
            jnp.bfloat16
        )
        acc_in = acc_in + lax.dot_general(
            rows_x, dpre, (((0,), (0,)), ((), ())), preferred_element_type=jnp.float32
        )
        acc_out = acc_out + lax.dot_general(
            scaled, rows_y, (((0,), (0,)), ((), ())), preferred_element_type=jnp.float32
        )
        dx_part = lax.dot_general(
            dpre, weight_in, (((1,), (1,)), ((), ())), preferred_element_type=jnp.float32
        ).astype(jnp.bfloat16)
        back_x, back_g = (
            lax.all_to_all(
                dx_part.reshape(dev_count, CAP, part), "dp", split_axis=0, concat_axis=0, tiled=True
            ),
            lax.all_to_all(
                block_sum.reshape(dev_count, CAP), "dp", split_axis=0, concat_axis=0, tiled=True
            ),
        )
        summed = jnp.sum(back_x.astype(jnp.float32).reshape(groups, 4, CAP, part), axis=0)
        dxs = summed.transpose(1, 0, 2).reshape(CAP, width)
        dgate = jnp.sum(back_g.astype(jnp.float32), axis=0)
        dxe = lax.dot_general(table, dxs, (((0,), (0,)), ((), ())), precision=hi)
        dg_tok = lax.dot_general(table, dgate, (((0,), (0,)), ((), ())), precision=hi)
        dlog = (dg_tok * prob[:, 0])[:, None] * (first[None, :] - prob)
        result = grad_in_tok.astype(jnp.float32) + dxe + jnp.dot(dlog, router_w.T, precision=hi)
        outputs.append(result.astype(jnp.bfloat16))
        router_term = jnp.dot(xf.T, dlog, precision=hi)
        acc_router = acc_router + lax.psum(router_term, "dp")
    input_grad = jnp.stack(outputs)[:, None]
    grad_in = acc_in.astype(jnp.bfloat16)[None, None]
    grad_out = acc_out.astype(jnp.bfloat16)[None, None]
    return (input_grad, grad_in, grad_out, acc_router[None])


def solution(mesh):
    in_specs = (
        P("section", None, "dp", None),
        P("section", "dp", None),
        P("dp", None),
        P("section", None, "dp", None),
        P(),
        P("section", None, None),
        P("section", "dp", None, None),
        P("section", "dp", None, None),
    )
    out_specs = (
        P(None, "section", "dp", None),
        P("section", "dp", None, None),
        P("section", "dp", None, None),
        P("section", None, None),
    )
    return jax.shard_map(local, mesh=mesh, in_specs=in_specs, out_specs=out_specs, check_vma=False)
```

profile of v0, /device:TPU:128, one launch (start us, length us, event | category | flops | bytes accessed | tf_op | source)
XLA Modules:
  0.0 1498.4 jit_solution(10897805153019167695)
XLA Ops:
  7.2 1.3 slice_bitcast_fusion.1
  8.5 1.3 dynamic_slice.3
  10.7 1.9 fusion.54
  12.9 1.3 broadcast_in_dim.22
  14.2 13.2 all-to-all-start.2
  27.6 23.9 %all-to-all-done.2 = bf16[128,2,1536]{2,1,0:T(2,128)(2,1)S(1)} async-done(((bf16[128,2,1536]{2,1,0:T(2,128)(2,1)}), bf16[128,2,1536]{2,1,0:T(2,128)(2,1)S(1)}, u32[]{:S(2)}, u32[]{:S(2)}) %all-to-all-start.2) | async-done | bytes 786464 | tf_op jit(solution)/shard_map/all_to_all | solution.py:92
  51.6 1.3 broadcast_in_dim.21
  52.9 7.2 all-to-all-start.1
  60.9 1.1 fusion.14
  62.0 1.9 collective-permute-start.2
  64.0 20.0 %all-to-all-done.1 = bf16[128,2,1536]{2,1,0:T(2,128)(2,1)} async-done(((bf16[128,2,1536]{2,1,0:T(2,128)(2,1)}), bf16[128,2,1536]{2,1,0:T(2,128)(2,1)}, u32[]{:S(2)}, u32[]{:S(2)}) %all-to-all-start.1) | async-done | bytes 786464 | tf_op jit(solution)/shard_map/all_to_all | solution.py:93
  83.9 2.3 reshape.242
  86.6 1.9 collective-permute-start
  89.8 1.9 collective-permute-start.3
  91.8 3.9 collective-permute-start.1
  96.6 6.1 all-to-all-start
  102.7 9.8 all-to-all-done
  114.4 1.8 multiply_reduce_fusion.1
  117.1 6.6 all-to-all-start.4
  123.7 1.3 convolution_convert_fusion.5
  125.0 1.2 reshape.246
  126.2 7.3 all-to-all-done.4
  133.5 6.2 all-to-all-start.3
  140.4 1.3 fusion.53
  141.7 1.4 reduce-window.17
  145.0 1.7 convolution_convert_fusion
  146.6 1.4 reshape.253
  148.0 1.4 copy.30
  149.4 14.5 all-to-all-done.3
  163.9 2.0 broadcast_in_dim.25
  165.9 6.2 all-to-all-start.7
  173.0 1.8 convert_reduce_fusion.1
  174.8 1.2 convolution_add_fusion.2
  176.0 1.7 fusion.1
  177.7 1.9 collective-permute-start.4
  179.7 9.9 collective-permute-done.4
  190.7 12.4 all-to-all-done.7
  203.2 1.3 broadcast_in_dim.24
  204.5 11.7 all-to-all-start.6
  216.2 1.4 fusion.56
  217.5 2.3 reshape.255
  221.0 1.9 collective-permute-start.7
  222.9 17.1 %all-to-all-done.6 = bf16[128,2,1536]{2,1,0:T(2,128)(2,1)} async-done(((bf16[128,2,1536]{2,1,0:T(2,128)(2,1)}), bf16[128,2,1536]{2,1,0:T(2,128)(2,1)}, u32[]{:S(2)}, u32[]{:S(2)}) %all-to-all-start.6) | async-done | bytes 786464 | tf_op jit(solution)/shard_map/all_to_all | solution.py:93
  240.0 3.0 reshape.252
  242.9 1.8 fusion.16
  244.7 1.9 collective-permute-start.5
  246.8 1.8 add.99
  248.6 1.9 collective-permute-start.8
  251.3 3.9 collective-permute-start.6
  255.4 15.5 %all_to_all.54 = bf16[128,1,2]{2,1,0:T(2,128)(2,1)S(1)} all-to-all(bf16[128,1,2]{2,1,0:T(2,128)(2,1)S(1)} %broadcast_in_dim.23), channel_id=1, replica_groups=mesh['dp'=128,'section'=4] {'dp'}, dimensions={0} | all-to-all | bytes 1024 | tf_op jit(solution)/shard_map/all_to_all | solution.py:94
  271.8 2.0 multiply_reduce_fusion
  274.6 6.1 all-to-all-start.9
  280.7 2.2 convolution_convert_fusion.4
  282.9 2.8 reshape.256
  285.7 4.9 all-to-all-done.9
  290.6 7.5 all-to-all-start.8
  299.5 1.7 fusion.27
  301.2 1.3 fusion.4
  303.4 1.3 fusion.5
  306.1 15.8 %all-to-all-done.8 = bf16[128,2,1536]{2,1,0:T(2,128)(2,1)} async-done(((bf16[128,2,1536]{2,1,0:T(2,128)(2,1)}), bf16[128,2,1536]{2,1,0:T(2,128)(2,1)}, u32[]{:S(2)}, u32[]{:S(2)}) %all-to-all-start.8) | async-done | bytes 786464 | tf_op jit(solution)/shard_map/all_to_all | solution.py:124
  321.9 1.8 convert_reduce_fusion
  324.0 1.3 fusion.30
  327.1 1162.6 %all-reduce.2.cloned.1.call-done = f32[6144,8]{0,1:T(8,128)} async-done(((f32[6144,8]{0,1:T(8,128)}), f32[6144,8]{0,1:T(8,128)}) %all-reduce.2.cloned.1.call-update) | async-done | bytes 196624 | tf_op jit(solution)/shard_map/psum | solution.py:140
  1489.7 1.6 copy.48
  (117 shorter events, 19.9 us)
Async XLA Ops:
  7.2 53.7 %copy-start = (bf16[1,1,1536,256]{3,2,1,0:T(8,128)(2,1)S(1)}, bf16[1,1,1536,256]{3,2,1,0:T(8,128)(2,1)}, u32[]{:S(2)}) copy-start(bf16[1,1,1536,256]{3,2,1,0:T(8,128)(2,1)} %param.14) | copy-start | bytes 2359300
  10.7 16.7 %copy-start.12 = (bf16[1,6,6144]{2,1,0:T(8,128)(2,1)S(1)}, bf16[1,6,6144]{2,1,0:T(8,128)(2,1)}, u32[]{:S(2)}) copy-start(bf16[1,6,6144]{2,1,0:T(8,128)(2,1)} %param.9) | copy-start | bytes 221188
  12.7 83.1 %copy-start.21 = (pred[2,6]{1,0:T(4,128)(4,1)}, pred[2,6]{1,0:T(4,128)(4,1)S(1)}, u32[]{:S(2)}) copy-start(pred[2,6]{1,0:T(4,128)(4,1)S(1)} %compare_and_fusion.1) | copy-start | bytes 40
  14.2 37.4 %all-to-all-start.2 = ((bf16[128,2,1536]{2,1,0:T(2,128)(2,1)}), bf16[128,2,1536]{2,1,0:T(2,128)(2,1)S(1)}, u32[]{:S(2)}, u32[]{:S(2)}) async-start(bf16[128,2,1536]{2,1,0:T(2,128)(2,1)} %bitcast.12), calls=%async_computation.2 | async-start | bytes 1572864 | tf_op jit(solution)/shard_map/all_to_all | solution.py:92
  27.4 32.7 %copy-start.4 = (f32[1,6144,8]{1,2,0:T(8,128)S(1)}, f32[1,6144,8]{1,2,0:T(8,128)}, u32[]{:S(2)}) copy-start(f32[1,6144,8]{1,2,0:T(8,128)} %param.13) | copy-start | bytes 589828
  52.9 31.1 %all-to-all-start.1 = ((bf16[128,2,1536]{2,1,0:T(2,128)(2,1)}), bf16[128,2,1536]{2,1,0:T(2,128)(2,1)}, u32[]{:S(2)}, u32[]{:S(2)}) async-start(bf16[128,2,1536]{2,1,0:T(2,128)(2,1)} %bitcast.9), calls=%async_computation.1 | async-start | bytes 1572864 | tf_op jit(solution)/shard_map/all_to_all | solution.py:93
  60.9 25.3 %copy-start.1 = (bf16[1,1,256,1536]{3,2,1,0:T(8,128)(2,1)S(1)}, bf16[1,1,256,1536]{3,2,1,0:T(8,128)(2,1)}, u32[]{:S(2)}) copy-start(bf16[1,1,256,1536]{3,2,1,0:T(8,128)(2,1)} %param.15) | copy-start | bytes 2359300
  62.0 26.7 %collective-permute-start.2 = (f32[256,256]{0,1:T(8,128)}, f32[256,256]{0,1:T(8,128)}, u32[]{:S(2)}, u32[]{:S(2)}) collective-permute-start(f32[256,256]{0,1:T(8,128)} %fusion.14), channel_id=1, source_target_pairs={{0,4},{4,0},{8,12},{12,8},{16,20},{20,16},{24,28},{28,24},{32,36},... | collective-permute-start | bytes 786440 | tf_op jit(solution)/shard_map/ppermute | solution.py:23
  86.6 5.1 collective-permute-start
  88.6 3.2 copy-start.14
  88.7 7.2 copy-start.26
  89.8 33.9 %copy-start.5 = (f32[256,256]{0,1:T(8,128)}, f32[256,256]{0,1:T(8,128)S(1)}, u32[]{:S(2)}) copy-start(f32[256,256]{0,1:T(8,128)S(1)} %add.89) | copy-start | bytes 786436
  89.8 24.5 %collective-permute-start.3 = (f32[256,256]{0,1:T(8,128)S(1)}, f32[256,256]{0,1:T(8,128)S(1)}, u32[]{:S(2)}, u32[]{:S(2)}) collective-permute-start(f32[256,256]{0,1:T(8,128)S(1)} %add.89), channel_id=1, source_target_pairs={{0,8},{8,0},{4,12},{12,4},{16,24},{24,16},{20,28},{28,20},{32,40},... | collective-permute-start | bytes 786440 | tf_op jit(solution)/shard_map/ppermute | solution.py:23
  91.8 22.6 %collective-permute-start.1 = (f32[256,256]{0,1:T(8,128)S(1)}, f32[256,256]{0,1:T(8,128)}, u32[]{:S(2)}, u32[]{:S(2)}) collective-permute-start(f32[256,256]{0,1:T(8,128)S(1)} %add.87), channel_id=1, source_target_pairs={{0,8},{8,0},{4,12},{12,4},{16,24},{24,16},{20,28},{28,20},{32,40},... | collective-permute-start | bytes 786440 | tf_op jit(solution)/shard_map/ppermute | solution.py:23
  96.6 16.0 %all-to-all-start = ((bf16[128,1,2]{2,1,0:T(2,128)(2,1)}), bf16[128,1,2]{2,1,0:T(2,128)(2,1)S(1)}, u32[]{:S(2)}, u32[]{:S(2)}) async-start(bf16[128,1,2]{2,1,0:T(2,128)(2,1)} %broadcast_in_dim.20), calls=%async_computation | async-start | bytes 131072 | tf_op jit(solution)/shard_map/all_to_all | solution.py:94
  114.4 2.7 copy-start.17
  114.4 9.3 copy-start.10
  117.1 16.5 %all-to-all-start.4 = ((bf16[128,1,2]{2,1,0:T(2,128)(2,1)}), bf16[128,1,2]{2,1,0:T(2,128)(2,1)S(1)}, u32[]{:S(2)}, u32[]{:S(2)}) async-start(bf16[128,1,2]{2,1,0:T(2,128)(2,1)} %convert_element_type.182), calls=%async_computation.4 | async-start | bytes 131072 | tf_op jit(solution)/shard_map/all_to_all | solution.py:127
  133.5 30.4 %all-to-all-start.3 = ((bf16[128,2,1536]{2,1,0:T(2,128)(2,1)}), bf16[128,2,1536]{2,1,0:T(2,128)(2,1)S(1)}, u32[]{:S(2)}, u32[]{:S(2)}) async-start(bf16[128,2,1536]{2,1,0:T(2,128)(2,1)} %reshape.246), calls=%async_computation.3 | async-start | bytes 1572864 | tf_op jit(solution)/shard_map/all_to_all | solution.py:124
  144.4 0.6 copy-start.22
  163.9 2.0 copy-start.3
  165.9 37.3 %all-to-all-start.7 = ((bf16[128,2,1536]{2,1,0:T(2,128)(2,1)}), bf16[128,2,1536]{2,1,0:T(2,128)(2,1)S(1)}, u32[]{:S(2)}, u32[]{:S(2)}) async-start(bf16[128,2,1536]{2,1,0:T(2,128)(2,1)} %bitcast.137), calls=%async_computation.7 | async-start | bytes 1572864 | tf_op jit(solution)/shard_map/all_to_all | solution.py:92
  172.1 5.6 copy-start.19
  172.3 17.3 %copy-start.23 = (pred[2,6]{1,0:T(4,128)(4,1)S(1)}, pred[2,6]{1,0:T(4,128)(4,1)}, u32[]{:S(2)}) copy-start(pred[2,6]{1,0:T(4,128)(4,1)} %copy-done.22) | copy-start | bytes 40
  173.0 6.6 copy-start.25
  177.7 11.9 collective-permute-start.4
  203.2 13.0 copy-start.2
  204.5 35.5 %all-to-all-start.6 = ((bf16[128,2,1536]{2,1,0:T(2,128)(2,1)}), bf16[128,2,1536]{2,1,0:T(2,128)(2,1)}, u32[]{:S(2)}, u32[]{:S(2)}) async-start(bf16[128,2,1536]{2,1,0:T(2,128)(2,1)} %bitcast.138), calls=%async_computation.6 | async-start | bytes 1572864 | tf_op jit(solution)/shard_map/all_to_all | solution.py:93
  221.0 25.9 %collective-permute-start.7 = (f32[256,256]{0,1:T(8,128)}, f32[256,256]{0,1:T(8,128)}, u32[]{:S(2)}, u32[]{:S(2)}) collective-permute-start(f32[256,256]{0,1:T(8,128)} %fusion.11), channel_id=1, source_target_pairs={{0,4},{4,0},{8,12},{12,8},{16,20},{20,16},{24,28},{28,24},{32,36},... | collective-permute-start | bytes 786440 | tf_op jit(solution)/shard_map/ppermute | solution.py:23
  244.7 5.8 collective-permute-start.5
  246.7 24.2 %copy-start.15 = (f32[6,8]{1,0:T(8,128)}, f32[6,8]{1,0:T(8,128)S(1)}, u32[]{:S(2)}) copy-start(f32[6,8]{1,0:T(8,128)S(1)} %broadcast_divide_fusion) | copy-start | bytes 580
  246.8 8.6 copy-start.27
  248.6 23.2 %collective-permute-start.8 = (f32[256,256]{0,1:T(8,128)}, f32[256,256]{0,1:T(8,128)}, u32[]{:S(2)}, u32[]{:S(2)}) collective-permute-start(f32[256,256]{0,1:T(8,128)} %add.99), channel_id=1, source_target_pairs={{0,8},{8,0},{4,12},{12,4},{16,24},{24,16},{20,28},{28,20},{32,40},... | collective-permute-start | bytes 786440 | tf_op jit(solution)/shard_map/ppermute | solution.py:23
  251.3 20.5 %collective-permute-start.6 = (f32[256,256]{0,1:T(8,128)}, f32[256,256]{0,1:T(8,128)}, u32[]{:S(2)}, u32[]{:S(2)}) collective-permute-start(f32[256,256]{0,1:T(8,128)} %add.97), channel_id=1, source_target_pairs={{0,8},{8,0},{4,12},{12,4},{16,24},{24,16},{20,28},{28,20},{32,40},... | collective-permute-start | bytes 786440 | tf_op jit(solution)/shard_map/ppermute | solution.py:23
  274.6 16.0 %all-to-all-start.9 = ((bf16[128,1,2]{2,1,0:T(2,128)(2,1)}), bf16[128,1,2]{2,1,0:T(2,128)(2,1)S(1)}, u32[]{:S(2)}, u32[]{:S(2)}) async-start(bf16[128,1,2]{2,1,0:T(2,128)(2,1)} %convert_element_type.183), calls=%async_computation.9 | async-start | bytes 131072 | tf_op jit(solution)/shard_map/all_to_all | solution.py:127
  290.6 31.3 %all-to-all-start.8 = ((bf16[128,2,1536]{2,1,0:T(2,128)(2,1)}), bf16[128,2,1536]{2,1,0:T(2,128)(2,1)}, u32[]{:S(2)}, u32[]{:S(2)}) async-start(bf16[128,2,1536]{2,1,0:T(2,128)(2,1)} %reshape.256), calls=%async_computation.8 | async-start | bytes 1572864 | tf_op jit(solution)/shard_map/all_to_all | solution.py:124
  298.1 1191.6 %all-reduce.2.cloned.1.call-start = ((), (), s32[]{:S(2)}) async-start(), calls=%async_computation.10 | async-start | bytes 393216 | tf_op jit(solution)/shard_map/psum | solution.py:140
  298.4 2.8 copy-start.6
  298.4 2.8 copy-start.11
  298.4 2.8 copy-start.18
  301.2 1.3 copy-start.9
  302.5 0.9 copy-start.8
  303.4 1.5 copy-start.24
  303.4 1.5 copy-start.28
  303.4 1.6 copy-start.7
  303.4 1.6 copy-start.16
  303.4 1.6 copy-start.20
  304.7 19.3 %copy-start.13 = (bf16[6,6144]{1,0:T(8,128)(2,1)S(1)}, bf16[6,6144]{1,0:T(8,128)(2,1)}, u32[]{:S(2)}) copy-start(bf16[6,6144]{1,0:T(8,128)(2,1)} %param.10) | copy-start | bytes 221188
Sparse Core Ops, SparseCore 0:
  306.2 1183.4 all-reduce.1
where the time goes:
time: 1510 us; the launch traced here: 1500 us
  waiting for transfers between devices  1300 us (86%)
  starting transfers between devices  92.4 us (6%)
  local copies, waits for them, and re-layouts  33 us (2%)
  matrix products  25.1 us (2%)
  other arithmetic  17.6 us (1%)
  between operations  16.3 us (1%)
  blocking collectives  15.5 us (1%)
    psum x1, waiting for transfers between devices, local(): acc_router = acc_router + lax.psum(router_term, 'dp')  1160 us
    all_to_all x2, waiting for transfers between devices, local(): lax.all_to_all(ysend, 'dp', split_axis=0, concat_axis=0, tiled=True)  37.1 us
    all_to_all x2, waiting for transfers between devices, local(): lax.all_to_all(xsend, 'dp', split_axis=0, concat_axis=0, tiled=True)  36.4 us
    all_to_all x2, waiting for transfers between devices, local(): lax.all_to_all(dx_part.reshape(dev_count, CAP, part), 'dp', split_axis=0,...  30.3 us
  transfers between devices with their start and end apart: 19, of which 11 were waited for; matrix products, arithmetic and copies ran while one was open for 4% of the time, Pallas kernels for 0%

commit v1 on v0

--- a/solution.py
+++ b/solution.py
@@ -137,7 +137,7 @@
         result = grad_in_tok.astype(jnp.float32) + dxe + jnp.dot(dlog, router_w.T, precision=hi)
         outputs.append(result.astype(jnp.bfloat16))
         router_term = jnp.dot(xf.T, dlog, precision=hi)
-        acc_router = acc_router + lax.psum(router_term, "dp")
+        acc_router = acc_router + jnp.sum(lax.all_gather(router_term, "dp"), 0)
     input_grad = jnp.stack(outputs)[:, None]
     grad_in = acc_in.astype(jnp.bfloat16)[None, None]
     grad_out = acc_out.astype(jnp.bfloat16)[None, None]

time: 1510 us -> 675 us (0.45)
  the two profiles are of different devices: /device:TPU:128 before, /device:TPU:1 now
where the time goes in v1:
time: 675 us; the launch traced here: 665 us
  waiting for transfers between devices  420 us (62%)
  starting transfers between devices  106 us (16%)
  blocking collectives  40.8 us (6%)
  other arithmetic  32.7 us (5%)
  local copies, waits for them, and re-layouts  24.9 us (4%)
  matrix products  23.7 us (4%)
  between operations  16.4 us (2%)
    all_gather x2, waiting for transfers between devices, local(): acc_router = acc_router + jnp.sum(lax.all_gather(router_term, 'dp'), 0)  275 us
    all_to_all x2, waiting for transfers between devices, local(): lax.all_to_all(dx_part.reshape(dev_count, CAP, part), 'dp', split_axis=0,...  41.8 us
    all_to_all x2, waiting for transfers between devices, local(): lax.all_to_all(ysend, 'dp', split_axis=0, concat_axis=0, tiled=True)  41.6 us
    all_to_all x2, starting transfers between devices, local(): lax.all_to_all(ysend, 'dp', split_axis=0, concat_axis=0, tiled=True)  37.3 us
    all_to_all x2, waiting for transfers between devices, local(): lax.all_to_all(xsend, 'dp', split_axis=0, concat_axis=0, tiled=True)  31.6 us
    ppermute x8, starting transfers between devices, from_partner(): return lax.ppermute(block, axis, route)  23.7 us
    all_to_all x1, blocking collectives, local(): lax.all_to_all(gsend, 'dp', split_axis=0, concat_axis=0, tiled=True)  22.3 us
    all_to_all x1, blocking collectives, local(): lax.all_to_all(block_sum.reshape(dev_count, CAP), 'dp', split_axis=0, con...  18.5 us
  transfers between devices with their start and end apart: 19, of which 11 were waited for; matrix products, arithmetic and copies ran while one was open for 9% of the time, Pallas kernels for 0%

profile of v1, /device:TPU:1, one launch (start us, length us, event | category | flops | bytes accessed | tf_op | source)
XLA Modules:
  0.0 665.0 jit_solution(13142066124567442609)
XLA Ops:
  7.2 1.4 slice_bitcast_fusion.1
  8.6 1.3 dynamic_slice.3
  10.8 1.1 convolution_convert_fusion.3
  11.9 1.3 broadcast_in_dim.19
  13.2 13.8 %all-to-all-start.1 = ((bf16[128,2,1536]{2,1,0:T(2,128)(2,1)}), bf16[128,2,1536]{2,1,0:T(2,128)(2,1)S(1)}, u32[]{:S(2)}, u32[]{:S(2)}) async-start(bf16[128,2,1536]{2,1,0:T(2,128)(2,1)} %bitcast.9), calls=%async_computation.1 | async-start | bytes 1572864 | tf_op jit(solution)/shard_map/all_to_all | solution.py:93
  27.5 23.4 %all-to-all-done.1 = bf16[128,2,1536]{2,1,0:T(2,128)(2,1)S(1)} async-done(((bf16[128,2,1536]{2,1,0:T(2,128)(2,1)}), bf16[128,2,1536]{2,1,0:T(2,128)(2,1)S(1)}, u32[]{:S(2)}, u32[]{:S(2)}) %all-to-all-start.1) | async-done | bytes 786464 | tf_op jit(solution)/shard_map/all_to_all | solution.py:93
  50.9 1.3 broadcast_in_dim.20
  52.2 7.5 %all-to-all-start.2 = ((bf16[128,2,1536]{2,1,0:T(2,128)(2,1)}), bf16[128,2,1536]{2,1,0:T(2,128)(2,1)}, u32[]{:S(2)}, u32[]{:S(2)}) async-start(bf16[128,2,1536]{2,1,0:T(2,128)(2,1)} %bitcast.12), calls=%async_computation.2 | async-start | bytes 1572864 | tf_op jit(solution)/shard_map/all_to_all | solution.py:92
  60.9 3.0 collective-permute-start
  63.9 19.5 %all-to-all-done.2 = bf16[128,2,1536]{2,1,0:T(2,128)(2,1)} async-done(((bf16[128,2,1536]{2,1,0:T(2,128)(2,1)}), bf16[128,2,1536]{2,1,0:T(2,128)(2,1)}, u32[]{:S(2)}, u32[]{:S(2)}) %all-to-all-start.2) | async-done | bytes 786464 | tf_op jit(solution)/shard_map/all_to_all | solution.py:92
  83.3 2.3 reshape.257
  86.1 3.1 collective-permute-start.2
  89.4 1.0 add.93
  90.4 1.9 collective-permute-start.1
  92.4 3.4 collective-permute-start.3
  96.6 5.7 all-to-all-start
  102.4 10.1 %all-to-all-done = bf16[128,1,2]{2,1,0:T(2,128)(2,1)S(1)} async-done(((bf16[128,1,2]{2,1,0:T(2,128)(2,1)}), bf16[128,1,2]{2,1,0:T(2,128)(2,1)S(1)}, u32[]{:S(2)}, u32[]{:S(2)}) %all-to-all-start) | async-done | bytes 544 | tf_op jit(solution)/shard_map/all_to_all | solution.py:94
  112.8 1.8 multiply_reduce_fusion.1
  115.4 6.4 all-to-all-start.4
  121.9 10.0 %all-to-all-done.4 = bf16[128,1,2]{2,1,0:T(2,128)(2,1)S(1)} async-done(((bf16[128,1,2]{2,1,0:T(2,128)(2,1)}), bf16[128,1,2]{2,1,0:T(2,128)(2,1)S(1)}, u32[]{:S(2)}, u32[]{:S(2)}) %all-to-all-start.4) | async-done | bytes 544 | tf_op jit(solution)/shard_map/all_to_all | solution.py:127
  132.2 1.0 convolution_bitcast_fusion.1
  133.3 1.3 convolution_convert_fusion.5
  134.6 1.2 reshape.258
  135.8 5.9 all-to-all-start.3
  142.9 22.8 %all-to-all-done.3 = bf16[128,2,1536]{2,1,0:T(2,128)(2,1)S(1)} async-done(((bf16[128,2,1536]{2,1,0:T(2,128)(2,1)}), bf16[128,2,1536]{2,1,0:T(2,128)(2,1)S(1)}, u32[]{:S(2)}, u32[]{:S(2)}) %all-to-all-start.3) | async-done | bytes 786464 | tf_op jit(solution)/shard_map/all_to_all | solution.py:124
  165.7 1.3 broadcast_in_dim.23
  167.0 10.9 %all-to-all-start.7 = ((bf16[128,2,1536]{2,1,0:T(2,128)(2,1)}), bf16[128,2,1536]{2,1,0:T(2,128)(2,1)S(1)}, u32[]{:S(2)}, u32[]{:S(2)}) async-start(bf16[128,2,1536]{2,1,0:T(2,128)(2,1)} %bitcast.144), calls=%async_computation.7 | async-start | bytes 1572864 | tf_op jit(solution)/shard_map/all_to_all | solution.py:92
  177.9 1.8 convert_reduce_fusion.1
  179.7 1.2 convolution_add_fusion.1
  180.9 1.0 fusion
  181.9 1.3 collective-permute-start.4
  183.2 10.4 %collective-permute-done.4 = bf16[6,6144]{1,0:T(8,128)(2,1)} collective-permute-done((bf16[6,6144]{1,0:T(8,128)(2,1)}, bf16[6,6144]{1,0:T(8,128)(2,1)}, u32[]{:S(2)}, u32[]{:S(2)}) %collective-permute-start.4) | collective-permute-done | bytes 73760 | tf_op jit(solution)/shard_map/ppermute | solution.py:13
  193.7 1.0 convolution_convert_fusion.1
  194.8 12.1 %all-to-all-done.7 = bf16[128,2,1536]{2,1,0:T(2,128)(2,1)S(1)} async-done(((bf16[128,2,1536]{2,1,0:T(2,128)(2,1)}), bf16[128,2,1536]{2,1,0:T(2,128)(2,1)S(1)}, u32[]{:S(2)}, u32[]{:S(2)}) %all-to-all-start.7) | async-done | bytes 786464 | tf_op jit(solution)/shard_map/all_to_all | solution.py:92
  206.9 1.3 broadcast_in_dim.22
  208.2 23.5 %all-to-all-start.6 = ((bf16[128,2,1536]{2,1,0:T(2,128)(2,1)}), bf16[128,2,1536]{2,1,0:T(2,128)(2,1)}, u32[]{:S(2)}, u32[]{:S(2)}) async-start(bf16[128,2,1536]{2,1,0:T(2,128)(2,1)} %bitcast.145), calls=%async_computation.6 | async-start | bytes 1572864 | tf_op jit(solution)/shard_map/all_to_all | solution.py:93
  232.3 2.3 reshape.267
  234.6 1.1 fusion.10
  235.8 2.9 collective-permute-start.7
  238.6 18.2 %all-to-all-done.6 = bf16[128,2,1536]{2,1,0:T(2,128)(2,1)} async-done(((bf16[128,2,1536]{2,1,0:T(2,128)(2,1)}), bf16[128,2,1536]{2,1,0:T(2,128)(2,1)}, u32[]{:S(2)}, u32[]{:S(2)}) %all-to-all-start.6) | async-done | bytes 786464 | tf_op jit(solution)/shard_map/all_to_all | solution.py:93
  256.9 3.0 reshape.264
  259.8 1.8 fusion.15
  261.6 1.9 collective-permute-start.5
  263.8 1.8 add.105
  265.5 5.6 collective-permute-start.8
  271.9 1.9 collective-permute-start.6
  274.0 22.3 %all_to_all.54 = bf16[128,1,2]{2,1,0:T(2,128)(2,1)S(1)} all-to-all(bf16[128,1,2]{2,1,0:T(2,128)(2,1)S(1)} %broadcast_in_dim.21), channel_id=1, replica_groups=mesh['dp'=128,'section'=4] {'dp'}, dimensions={0} | all-to-all | bytes 1024 | tf_op jit(solution)/shard_map/all_to_all | solution.py:94
  297.2 2.0 multiply_reduce_fusion
  300.5 18.5 %all_to_all.55 = bf16[128,1,2]{2,1,0:T(2,128)(2,1)S(1)} all-to-all(bf16[128,1,2]{2,1,0:T(2,128)(2,1)S(1)} %convert_element_type.183), channel_id=1, replica_groups=mesh['dp'=128,'section'=4] {'dp'}, dimensions={0} | all-to-all | bytes 1024 | tf_op jit(solution)/shard_map/all_to_all | solution.py:127
  319.9 1.7 convolution_bitcast_fusion
  321.6 2.2 convolution_convert_fusion.4
  323.8 2.9 reshape.268
  326.8 7.1 %all-to-all-start.8 = ((bf16[128,2,1536]{2,1,0:T(2,128)(2,1)}), bf16[128,2,1536]{2,1,0:T(2,128)(2,1)}, u32[]{:S(2)}, u32[]{:S(2)}) async-start(bf16[128,2,1536]{2,1,0:T(2,128)(2,1)} %reshape.268), calls=%async_computation.8 | async-start | bytes 1572864 | tf_op jit(solution)/shard_map/all_to_all | solution.py:124
  333.9 1.5 fusion.26
  335.4 2.3 fusion.3
  338.6 1.3 fusion.4
  339.9 19.0 %all-to-all-done.8 = bf16[128,2,1536]{2,1,0:T(2,128)(2,1)} async-done(((bf16[128,2,1536]{2,1,0:T(2,128)(2,1)}), bf16[128,2,1536]{2,1,0:T(2,128)(2,1)}, u32[]{:S(2)}, u32[]{:S(2)}) %all-to-all-start.8) | async-done | bytes 786464 | tf_op jit(solution)/shard_map/all_to_all | solution.py:124
  358.9 1.8 convert_reduce_fusion
  361.1 1.3 fusion.29
  362.3 0.9 maximum_bitcast_fusion
  364.1 47.9 %all-gather.5.cloned.1.call-done = f32[786432,8]{0,1:T(8,128)} async-done(((f32[6144,8]{0,1:T(8,128)}), f32[786432,8]{0,1:T(8,128)}) %all-gather.5.cloned.1.call-update) | async-done | bytes 25165840 | tf_op jit(solution)/shard_map/all_gather | solution.py:140
  412.0 9.2 %reduce_sum.98 = f32[6144,8]{0,1:T(8,128)S(1)} reduce(f32[128,6144,8]{1,2,0:T(8,128)} %bitcast.141, f32[]{:T(128)} %constant.43.clone.1), dimensions={0}, to_apply=%region_10.11 | reduce | flops 6242304 | bytes 25362436 | tf_op jit(solution)/shard_map/reduce_sum | solution.py:140
  421.2 226.9 %all-gather.7.cloned.1.call-done = f32[786432,8]{0,1:T(8,128)} async-done(((f32[6144,8]{0,1:T(8,128)}), f32[786432,8]{0,1:T(8,128)}) %all-gather.7.cloned.1.call-update) | async-done | bytes 25165840 | tf_op jit(solution)/shard_map/all_gather | solution.py:140
  648.1 9.2 %reduce_sum.99 = f32[6144,8]{0,1:T(8,128)S(1)} reduce(f32[128,6144,8]{1,2,0:T(8,128)} %bitcast.142, f32[]{:T(128)} %constant.43.clone.1), dimensions={0}, to_apply=%region_11.12 | reduce | flops 6242304 | bytes 25362436 | tf_op jit(solution)/shard_map/reduce_sum | solution.py:140
  (125 shorter events, 12.9 us)
Async XLA Ops:
  7.2 78.5 %copy-start = (bf16[1,1,1536,256]{3,2,1,0:T(8,128)(2,1)S(1)}, bf16[1,1,1536,256]{3,2,1,0:T(8,128)(2,1)}, u32[]{:S(2)}) copy-start(bf16[1,1,1536,256]{3,2,1,0:T(8,128)(2,1)} %param.14) | copy-start | bytes 2359300
  7.2 19.8 %copy-start.13 = (bf16[1,2,6,6144]{3,1,2,0:T(2,128)(2,1)S(1)}, bf16[1,2,6,6144]{3,1,2,0:T(2,128)(2,1)}, u32[]{:S(2)}) copy-start(bf16[1,2,6,6144]{3,1,2,0:T(2,128)(2,1)} %param.8) | copy-start | bytes 442372
  10.8 85.0 %copy-start.25 = (pred[2,6]{1,0:T(4,128)(4,1)}, pred[2,6]{1,0:T(4,128)(4,1)S(1)}, u32[]{:S(2)}) copy-start(pred[2,6]{1,0:T(4,128)(4,1)S(1)} %compare_and_fusion.1) | copy-start | bytes 40
  13.2 37.7 %all-to-all-start.1 = ((bf16[128,2,1536]{2,1,0:T(2,128)(2,1)}), bf16[128,2,1536]{2,1,0:T(2,128)(2,1)S(1)}, u32[]{:S(2)}, u32[]{:S(2)}) async-start(bf16[128,2,1536]{2,1,0:T(2,128)(2,1)} %bitcast.9), calls=%async_computation.1 | async-start | bytes 1572864 | tf_op jit(solution)/shard_map/all_to_all | solution.py:93
  27.0 32.7 %copy-start.6 = (f32[1,6144,8]{1,2,0:T(8,128)S(1)}, f32[1,6144,8]{1,2,0:T(8,128)}, u32[]{:S(2)}) copy-start(f32[1,6144,8]{1,2,0:T(8,128)} %param.13) | copy-start | bytes 589828
  27.3 32.4 %copy-start.9 = (bf16[1,1,6,6144]{3,1,2,0:T(2,128)(2,1)}, bf16[1,1,6,6144]{3,1,2,0:T(2,128)(2,1)S(1)}, u32[]{:S(2)}) copy-start(bf16[1,1,6,6144]{3,1,2,0:T(2,128)(2,1)S(1)} %get-tuple-element.24) | copy-start | bytes 221188
  52.1 8.3 %copy-start.3 = (bf16[1,1,256,1536]{3,2,1,0:T(8,128)(2,1)S(1)}, bf16[1,1,256,1536]{3,2,1,0:T(8,128)(2,1)}, u32[]{:S(2)}) copy-start(bf16[1,1,256,1536]{3,2,1,0:T(8,128)(2,1)} %param.15) | copy-start | bytes 2359300
  52.2 31.2 %all-to-all-start.2 = ((bf16[128,2,1536]{2,1,0:T(2,128)(2,1)}), bf16[128,2,1536]{2,1,0:T(2,128)(2,1)}, u32[]{:S(2)}, u32[]{:S(2)}) async-start(bf16[128,2,1536]{2,1,0:T(2,128)(2,1)} %bitcast.12), calls=%async_computation.2 | async-start | bytes 1572864 | tf_op jit(solution)/shard_map/all_to_all | solution.py:92
  60.9 28.5 %collective-permute-start = (f32[256,256]{0,1:T(8,128)S(1)}, f32[256,256]{0,1:T(8,128)}, u32[]{:S(2)}, u32[]{:S(2)}) collective-permute-start(f32[256,256]{0,1:T(8,128)S(1)} %fusion.17), channel_id=1, source_target_pairs={{0,4},{4,0},{8,12},{12,8},{16,20},{20,16},{24,28},{28,24},{32,36},... | collective-permute-start | bytes 786440 | tf_op jit(solution)/shard_map/ppermute | solution.py:23
  86.1 6.3 collective-permute-start.2
  89.3 42.9 %copy-start.15 = (f32[6,8]{1,0:T(8,128)}, f32[6,8]{1,0:T(8,128)S(1)}, u32[]{:S(2)}) copy-start(f32[6,8]{1,0:T(8,128)S(1)} %broadcast_divide_fusion.1) | copy-start | bytes 580
  89.4 42.8 %copy-start.10 = (bf16[1,1,6,6144]{3,1,2,0:T(2,128)(2,1)S(1)}, bf16[1,1,6,6144]{3,1,2,0:T(2,128)(2,1)}, u32[]{:S(2)}) copy-start(bf16[1,1,6,6144]{3,1,2,0:T(2,128)(2,1)} %copy-done.9) | copy-start | bytes 221188
  90.4 22.3 %collective-permute-start.1 = (f32[256,256]{0,1:T(8,128)S(1)}, f32[256,256]{0,1:T(8,128)}, u32[]{:S(2)}, u32[]{:S(2)}) collective-permute-start(f32[256,256]{0,1:T(8,128)S(1)} %add.93), channel_id=1, source_target_pairs={{0,8},{8,0},{4,12},{12,4},{16,24},{24,16},{20,28},{28,20},{32,40},... | collective-permute-start | bytes 786440 | tf_op jit(solution)/shard_map/ppermute | solution.py:23
  92.4 40.8 %copy-start.7 = (f32[256,256]{0,1:T(8,128)}, f32[256,256]{0,1:T(8,128)S(1)}, u32[]{:S(2)}) copy-start(f32[256,256]{0,1:T(8,128)S(1)} %add.95) | copy-start | bytes 786436
  92.4 20.4 %collective-permute-start.3 = (f32[256,256]{0,1:T(8,128)S(1)}, f32[256,256]{0,1:T(8,128)}, u32[]{:S(2)}, u32[]{:S(2)}) collective-permute-start(f32[256,256]{0,1:T(8,128)S(1)} %add.95), channel_id=1, source_target_pairs={{0,8},{8,0},{4,12},{12,4},{16,24},{24,16},{20,28},{28,20},{32,40},... | collective-permute-start | bytes 786440 | tf_op jit(solution)/shard_map/ppermute | solution.py:23
  95.9 36.1 %copy-start.26 = (pred[2,6]{1,0:T(4,128)(4,1)S(1)}, pred[2,6]{1,0:T(4,128)(4,1)}, u32[]{:S(2)}) copy-start(pred[2,6]{1,0:T(4,128)(4,1)} %copy-done.25) | copy-start | bytes 40
  96.6 15.8 %all-to-all-start = ((bf16[128,1,2]{2,1,0:T(2,128)(2,1)}), bf16[128,1,2]{2,1,0:T(2,128)(2,1)S(1)}, u32[]{:S(2)}, u32[]{:S(2)}) async-start(bf16[128,1,2]{2,1,0:T(2,128)(2,1)} %broadcast_in_dim.18), calls=%async_computation | async-start | bytes 131072 | tf_op jit(solution)/shard_map/all_to_all | solution.py:94
  112.8 20.5 %copy-start.20 = (f32[256]{0:T(256)}, f32[256]{0:T(256)S(1)}, u32[]{:S(2)}) copy-start(f32[256]{0:T(256)S(1)} %reshape.272) | copy-start | bytes 3076
  115.4 16.5 %all-to-all-start.4 = ((bf16[128,1,2]{2,1,0:T(2,128)(2,1)}), bf16[128,1,2]{2,1,0:T(2,128)(2,1)S(1)}, u32[]{:S(2)}, u32[]{:S(2)}) async-start(bf16[128,1,2]{2,1,0:T(2,128)(2,1)} %convert_element_type.182), calls=%async_computation.4 | async-start | bytes 131072 | tf_op jit(solution)/shard_map/all_to_all | solution.py:127
  121.8 290.2 %all-gather.5.cloned.1.call-start = ((), (), s32[]{:S(2)}) async-start(), calls=%async_computation.10 | async-start | bytes 25362432 | tf_op jit(solution)/shard_map/all_gather | solution.py:140
  121.9 59.0 %copy-start.22 = (f32[8]{0:T(128)}, f32[8]{0:T(128)S(1)}, u32[]{:S(2)}) copy-start(f32[8]{0:T(128)S(1)} %compare_convert_fusion) | copy-start | bytes 100
  134.6 7.8 %copy-start.24 = (s32[6,2]{0,1:T(2,128)S(1)}, s32[6,2]{0,1:T(2,128)}, u32[]{:S(2)}) copy-start(s32[6,2]{0,1:T(2,128)} %get-tuple-element.27) | copy-start | bytes 148
  135.8 29.9 %all-to-all-start.3 = ((bf16[128,2,1536]{2,1,0:T(2,128)(2,1)}), bf16[128,2,1536]{2,1,0:T(2,128)(2,1)S(1)}, u32[]{:S(2)}, u32[]{:S(2)}) async-start(bf16[128,2,1536]{2,1,0:T(2,128)(2,1)} %reshape.258), calls=%async_computation.3 | async-start | bytes 1572864 | tf_op jit(solution)/shard_map/all_to_all | solution.py:124
  142.6 131.2 %copy-start.28 = (pred[2,6]{1,0:T(4,128)(4,1)}, pred[2,6]{1,0:T(4,128)(4,1)S(1)}, u32[]{:S(2)}) copy-start(pred[2,6]{1,0:T(4,128)(4,1)S(1)} %compare_and_fusion) | copy-start | bytes 40
  142.9 36.8 %copy-start.27 = (pred[2,6]{1,0:T(4,128)(4,1)S(1)}, pred[2,6]{1,0:T(4,128)(4,1)}, u32[]{:S(2)}) copy-start(pred[2,6]{1,0:T(4,128)(4,1)} %copy-done.25) | copy-start | bytes 40
  165.7 1.3 copy-start.5
  166.9 14.0 %copy-start.16 = (f32[6,8]{1,0:T(8,128)S(1)}, f32[6,8]{1,0:T(8,128)}, u32[]{:S(2)}) copy-start(f32[6,8]{1,0:T(8,128)} %copy-done.15) | copy-start | bytes 580
  167.0 39.9 %all-to-all-start.7 = ((bf16[128,2,1536]{2,1,0:T(2,128)(2,1)}), bf16[128,2,1536]{2,1,0:T(2,128)(2,1)S(1)}, u32[]{:S(2)}, u32[]{:S(2)}) async-start(bf16[128,2,1536]{2,1,0:T(2,128)(2,1)} %bitcast.144), calls=%async_computation.7 | async-start | bytes 1572864 | tf_op jit(solution)/shard_map/all_to_all | solution.py:92
  181.9 11.7 %collective-permute-start.4 = (bf16[6,6144]{1,0:T(8,128)(2,1)}, bf16[6,6144]{1,0:T(8,128)(2,1)}, u32[]{:S(2)}, u32[]{:S(2)}) collective-permute-start(bf16[6,6144]{1,0:T(8,128)(2,1)} %fusion), channel_id=1, source_target_pairs={{1,0},{2,1},{3,2},{5,4},{6,5},{7,6},{9,8},{10,9},{11,10},{13,12},{... | collective-permute-start | bytes 221192 | tf_op jit(solution)/shard_map/ppermute | solution.py:13
  206.9 25.0 %copy-start.4 = (bf16[128,2,1536]{2,1,0:T(2,128)(2,1)}, bf16[128,2,1536]{2,1,0:T(2,128)(2,1)S(1)}, u32[]{:S(2)}) copy-start(bf16[128,2,1536]{2,1,0:T(2,128)(2,1)S(1)} %all-to-all-done.7) | copy-start | bytes 2359300
  208.2 48.7 %all-to-all-start.6 = ((bf16[128,2,1536]{2,1,0:T(2,128)(2,1)}), bf16[128,2,1536]{2,1,0:T(2,128)(2,1)}, u32[]{:S(2)}, u32[]{:S(2)}) async-start(bf16[128,2,1536]{2,1,0:T(2,128)(2,1)} %bitcast.145), calls=%async_computation.6 | async-start | bytes 1572864 | tf_op jit(solution)/shard_map/all_to_all | solution.py:93
  231.7 416.4 %all-gather.7.cloned.1.call-start = ((), (), s32[]{:S(2)}) async-start(), calls=%async_computation.11 | async-start | bytes 25362432 | tf_op jit(solution)/shard_map/all_gather | solution.py:140
  235.8 28.0 %collective-permute-start.7 = (f32[256,256]{0,1:T(8,128)}, f32[256,256]{0,1:T(8,128)}, u32[]{:S(2)}, u32[]{:S(2)}) collective-permute-start(f32[256,256]{0,1:T(8,128)} %fusion.10), channel_id=1, source_target_pairs={{0,4},{4,0},{8,12},{12,8},{16,20},{20,16},{24,28},{28,24},{32,36},... | collective-permute-start | bytes 786440 | tf_op jit(solution)/shard_map/ppermute | solution.py:23
  261.6 9.5 %collective-permute-start.5 = (f32[256,256]{0,1:T(8,128)S(1)}, f32[256,256]{0,1:T(8,128)S(1)}, u32[]{:S(2)}, u32[]{:S(2)}) collective-permute-start(f32[256,256]{0,1:T(8,128)S(1)} %fusion.15), channel_id=1, source_target_pairs={{0,4},{4,0},{8,12},{12,8},{16,20},{20,16},{24,28},{28,24},{32,36},... | collective-permute-start | bytes 786440 | tf_op jit(solution)/shard_map/ppermute | solution.py:23
  263.6 32.7 %copy-start.17 = (f32[6,8]{1,0:T(8,128)}, f32[6,8]{1,0:T(8,128)S(1)}, u32[]{:S(2)}) copy-start(f32[6,8]{1,0:T(8,128)S(1)} %broadcast_divide_fusion) | copy-start | bytes 580
  263.7 10.2 %copy-start.30 = (f32[6]{0:T(128)}, f32[6]{0:T(128)S(1)}, u32[]{:S(2)}) copy-start(f32[6]{0:T(128)S(1)} %slice_reduce_fusion) | copy-start | bytes 76
  265.5 31.6 %collective-permute-start.8 = (f32[256,256]{0,1:T(8,128)}, f32[256,256]{0,1:T(8,128)}, u32[]{:S(2)}, u32[]{:S(2)}) collective-permute-start(f32[256,256]{0,1:T(8,128)} %add.105), channel_id=1, source_target_pairs={{0,8},{8,0},{4,12},{12,4},{16,24},{24,16},{20,28},{28,20},{32,40},... | collective-permute-start | bytes 786440 | tf_op jit(solution)/shard_map/ppermute | solution.py:23
  271.9 25.3 %collective-permute-start.6 = (f32[256,256]{0,1:T(8,128)}, f32[256,256]{0,1:T(8,128)}, u32[]{:S(2)}, u32[]{:S(2)}) collective-permute-start(f32[256,256]{0,1:T(8,128)} %add.103), channel_id=1, source_target_pairs={{0,8},{8,0},{4,12},{12,4},{16,24},{24,16},{20,28},{28,20},{32,40},... | collective-permute-start | bytes 786440 | tf_op jit(solution)/shard_map/ppermute | solution.py:23
  323.8 10.1 %copy-start.2 = (bf16[256,1536]{1,0:T(8,128)(2,1)S(1)}, bf16[256,1536]{1,0:T(8,128)(2,1)}, u32[]{:S(2)}) copy-start(bf16[256,1536]{1,0:T(8,128)(2,1)} %reshape.264) | copy-start | bytes 2359300
  323.8 10.1 %copy-start.19 = (f32[256]{0:T(256)S(1)}, f32[256]{0:T(256)}, u32[]{:S(2)}) copy-start(f32[256]{0:T(256)} %reshape.275) | copy-start | bytes 3076
  326.8 32.2 %all-to-all-start.8 = ((bf16[128,2,1536]{2,1,0:T(2,128)(2,1)}), bf16[128,2,1536]{2,1,0:T(2,128)(2,1)}, u32[]{:S(2)}, u32[]{:S(2)}) async-start(bf16[128,2,1536]{2,1,0:T(2,128)(2,1)} %reshape.268), calls=%async_computation.8 | async-start | bytes 1572864 | tf_op jit(solution)/shard_map/all_to_all | solution.py:124
  333.9 1.5 copy-start.8
  333.9 1.5 copy-start.21
  335.4 2.3 copy-start.12
  337.7 0.9 copy-start.11
  338.6 22.1 %copy-start.29 = (pred[2,6]{1,0:T(4,128)(4,1)S(1)}, pred[2,6]{1,0:T(4,128)(4,1)}, u32[]{:S(2)}) copy-start(pred[2,6]{1,0:T(4,128)(4,1)} %copy-done.28) | copy-start | bytes 40
  338.6 22.4 %copy-start.14 = (bf16[6,6144]{1,0:T(8,128)(2,1)S(1)}, bf16[6,6144]{1,0:T(8,128)(2,1)}, u32[]{:S(2)}) copy-start(bf16[6,6144]{1,0:T(8,128)(2,1)} %param.10) | copy-start | bytes 221188
  338.6 22.4 %copy-start.18 = (f32[6,8]{1,0:T(8,128)S(1)}, f32[6,8]{1,0:T(8,128)}, u32[]{:S(2)}) copy-start(f32[6,8]{1,0:T(8,128)} %copy-done.17) | copy-start | bytes 580
  338.6 22.4 %copy-start.23 = (f32[8]{0:T(128)S(1)}, f32[8]{0:T(128)}, u32[]{:S(2)}) copy-start(f32[8]{0:T(128)} %copy-done.22) | copy-start | bytes 100
  648.1 9.9 %copy-start.1 = (bf16[1,1,1536,256]{3,2,1,0:T(8,128)(2,1)S(1)}, bf16[1,1,1536,256]{3,2,1,0:T(8,128)(2,1)}, u32[]{:S(2)}) copy-start(bf16[1,1,1536,256]{3,2,1,0:T(8,128)(2,1)} %param.14) | copy-start | bytes 2359300
Sparse Core Ops, SparseCore 0:
  133.4 278.5 all-gather.4
  414.1 233.8 all-gather.6
